TPU v7x, 32 devices: a whole 2x2x4 slice. The times are simulated.
32 devices in a mesh: dp: 8 (over z, x), ctx: 4 (over y, core).
Axes of the slice: x: 2, y: 2, z: 4, core: 2. Of those that a mesh axis runs over, the one named last changes fastest.
Arguments:
- inputs: bfloat16 [512, 16, 1024], P('ctx', 'dp'), may hold values from -6 to 6
- cotangent: bfloat16 [512, 16, 1024], P('ctx', 'dp'), may hold values from -6 to 6
- lengths: int32 [16], P('dp'), may hold values from 128 to 512, as said below
- block_order: int32 [8], replicated, may hold values from 0 to 7, as said below
- norm_gain: bfloat16 [1024], P('dp'), may hold values from 0.5 to 1.5
- norm_bias: bfloat16 [1024], P('dp'), may hold values from -1.75 to 1.75
- attend_weight: bfloat16 [1024, 3072], P('dp'), may hold values from -0.1875 to 0.1875
- attend_bias: bfloat16 [3072], P('dp'), may hold values from -3 to 3
- dense_weight: bfloat16 [1024, 1024], P('dp'), may hold values from -6 to 6
- dense_bias: bfloat16 [1024], P('dp'), may hold values from -3 to 3
- up_weight: bfloat16 [1024, 4096], P('dp'), may hold values from -0.1875 to 0.1875
- up_bias: bfloat16 [4096], P('dp'), may hold values from -3 to 3
- down_weight: bfloat16 [4096, 1024], P('dp'), may hold values from -0.09375 to 0.09375
- down_bias: bfloat16 [1024], P('dp'), may hold values from -3 to 3
Outputs:
- output: bfloat16 [512, 16, 1024], P('ctx', 'dp')
- input_grad: bfloat16 [512, 16, 1024], P('ctx', 'dp')
- grad_norm_gain: float32 [1024], P('dp')
- grad_norm_bias: float32 [1024], P('dp')
- grad_attend_weight: float32 [1024, 3072], P('dp')
- grad_attend_bias: float32 [3072], P('dp')
- grad_dense_weight: float32 [1024, 1024], P('dp')
- grad_dense_bias: float32 [1024], P('dp')
- grad_up_weight: float32 [1024, 4096], P('dp')
- grad_up_bias: float32 [4096], P('dp')
- grad_down_weight: float32 [4096, 1024], P('dp')
- grad_down_bias: float32 [1024], P('dp')
Inputs may be any that keep to these rules, and one draw needn't show every extreme that they name: Slots of sequence s whose position is lengths[s] or more are padding; in every draw some sequence has exactly 512 valid slots and some exactly 128. Each of 0 to 7 appears once, and block_order[2 c] + block_order[2 c + 1] = 7 for every c.
All inputs are finite; a program needn't handle non-finite values.
Results may differ from a plain program's by a relative error of at most 0.018.
Values may be sent and summed in bfloat16 or wider, within the bound.
No kernel may reach another device: no remote copies, remote signals or barrier semaphores. Data moves between devices by JAX's collectives and lax.ppermute only.
A program may use at most 320 MiB of HBM per device.

v0:
```python
import math
import jax
import jax.numpy as jnp
from jax import lax
from jax.sharding import PartitionSpec as P

HEADS = 16
HEAD_DIM = 64
ROT = 16
BLK = 64
EPSILON = 1e-05
ROOT_HALF = 0.7071067811865476
NORMAL_PEAK = 0.3989422804014327


def place_of(block_order, first_slot, count):
    slot = first_slot + jnp.arange(count, dtype=jnp.int32)
    which = slot // BLK
    table = jnp.arange(block_order.shape[0], dtype=jnp.int32)
    chosen = jnp.sum(jnp.where(which[:, None] == table[None, :], block_order[None, :], 0), axis=1)
    return chosen * BLK + slot % BLK


def angles(places):
    rates = 10000.0 ** (-jnp.arange(0, ROT, 2, dtype=jnp.float32) / ROT)
    turned = places.astype(jnp.float32)[:, None] * rates[None, :]
    doubled = jnp.concatenate([turned, turned], axis=-1)
    return (jnp.cos(doubled), jnp.sin(doubled))


def turn_half(values):
    half = values.shape[-1] // 2
    return jnp.concatenate([-values[..., half:], values[..., :half]], axis=-1)


def rotary(values, cosine, sine):
    front = values[..., :ROT]
    moved = front * cosine[:, None, None, :] + turn_half(front) * sine[:, None, None, :]
    return jnp.concatenate([moved, values[..., ROT:]], axis=-1)


def sweep(step_fn, carry, piece, start):
    count = jax.tree.leaves(piece)[0].shape[0]
    size = math.gcd(count, 512)
    if size == count:
        return step_fn(carry, piece, start)

    def inner(turn, state):
        part = jax.tree.map(
            lambda array: lax.dynamic_slice_in_dim(array, turn * size, size, 0), piece
        )
        return step_fn(state, part, start + turn * size)

    return lax.fori_loop(0, count // size, inner, carry)


def body(
    inputs,
    cotangent,
    lengths,
    block_order,
    norm_gain,
    norm_bias,
    attend_weight,
    attend_bias,
    dense_weight,
    dense_bias,
    up_weight,
    up_bias,
    down_weight,
    down_bias,
):
    local, sequences, width = inputs.shape
    rows = local * sequences
    scale = HEAD_DIM ** (-0.5)
    first_slot = lax.axis_index("ctx") * local
    places = place_of(block_order, first_slot, local)
    valid = (places[:, None] < lengths[None, :]).astype(jnp.float32)
    (
        gain,
        shift,
        attend_full,
        attend_shift,
        dense_full,
        dense_shift,
        up_full,
        up_shift,
        down_full,
        down_shift,
    ) = (
        lax.all_gather(norm_gain, "dp", axis=0, tiled=True),
        lax.all_gather(norm_bias, "dp", axis=0, tiled=True),
        lax.all_gather(attend_weight, "dp", axis=0, tiled=True),
        lax.all_gather(attend_bias, "dp", axis=0, tiled=True),
        lax.all_gather(dense_weight, "dp", axis=0, tiled=True),
        lax.all_gather(dense_bias, "dp", axis=0, tiled=True),
        lax.all_gather(up_weight, "dp", axis=0, tiled=True),
        lax.all_gather(up_bias, "dp", axis=0, tiled=True),
        lax.all_gather(down_weight, "dp", axis=0, tiled=True),
        lax.all_gather(down_bias, "dp", axis=0, tiled=True),
    )
    source = inputs.astype(jnp.float32)
    mean = jnp.mean(source, axis=-1, keepdims=True)
    centred = source - mean
    inverse = lax.rsqrt(jnp.mean(centred * centred, axis=-1, keepdims=True) + EPSILON)
    unit = centred * inverse
    normed_low = (
        (unit * gain.astype(jnp.float32) + shift.astype(jnp.float32))
        .astype(jnp.bfloat16)
        .reshape(rows, width)
    )
    projected = (
        jnp.dot(normed_low, attend_full, preferred_element_type=jnp.float32)
        + attend_shift.astype(jnp.float32)
    ).reshape(local, sequences, 3, HEADS, HEAD_DIM)
    cosine, sine = angles(places)
    queries = rotary(projected[:, :, 0], cosine, sine).astype(jnp.bfloat16)
    key_rot = rotary(projected[:, :, 1], cosine, sine).astype(jnp.bfloat16)
    value_low = projected[:, :, 2].astype(jnp.bfloat16)
    key_pairs = jnp.concatenate(
        [key_rot.reshape(local, sequences, width), value_low.reshape(local, sequences, width)],
        axis=-1,
    )

    def split_pairs(piece):
        count = piece.shape[0]
        return (
            piece[..., :width].reshape(count, sequences, HEADS, HEAD_DIM),
            piece[..., width:].reshape(count, sequences, HEADS, HEAD_DIM),
        )

    def exp_weights(piece, start):
        key_part, value_part = split_pairs(piece)
        key_places = place_of(block_order, start, piece.shape[0])
        scores = (
            jnp.einsum("qshd,kshd->shqk", queries, key_part, preferred_element_type=jnp.float32)
            * scale
        )
        allowed = key_places[None, :] <= places[:, None]
        return (jnp.where(allowed, jnp.exp(scores), 0.0), key_part, value_part)

    def forward_step(carry, piece, start):
        summed, total = carry
        weights, key_part, value_part = exp_weights(piece, start)
        summed = summed + jnp.einsum(
            "shqk,kshd->shqd",
            weights.astype(jnp.bfloat16),
            value_part,
            preferred_element_type=jnp.float32,
        )
        return (summed, total + jnp.sum(weights, axis=-1))

    start_carry = (
        jnp.zeros((sequences, HEADS, local, HEAD_DIM), jnp.float32),
        jnp.zeros((sequences, HEADS, local), jnp.float32),
    )
    summed, total = sweep(
        forward_step,
        start_carry,
        lax.all_gather(key_pairs, "ctx", axis=0, tiled=True),
        jnp.int32(0),
    )
    mixed = summed / total[..., None]
    mixed_low = jnp.transpose(mixed, (2, 0, 1, 3)).reshape(rows, width).astype(jnp.bfloat16)
    hidden = jnp.dot(normed_low, up_full, preferred_element_type=jnp.float32) + up_shift.astype(
        jnp.float32
    )
    active_low = jax.nn.gelu(hidden, approximate=False).astype(jnp.bfloat16)
    branch = (
        jnp.dot(mixed_low, dense_full, preferred_element_type=jnp.float32)
        + dense_shift.astype(jnp.float32)
        + jnp.dot(active_low, down_full, preferred_element_type=jnp.float32)
        + down_shift.astype(jnp.float32)
    )
    output = (valid[..., None] * (source + branch.reshape(local, sequences, width))).astype(
        jnp.bfloat16
    )
    pulled = valid[..., None] * cotangent.astype(jnp.float32)
    pulled_low = pulled.astype(jnp.bfloat16).reshape(rows, width)
    bias_grad = jnp.sum(pulled_low.astype(jnp.float32), axis=0)
    grad_dense = jnp.dot(mixed_low.T, pulled_low, preferred_element_type=jnp.float32)
    grad_down = jnp.dot(active_low.T, pulled_low, preferred_element_type=jnp.float32)
    slope = (
        0.5 * (1.0 + lax.erf(hidden * ROOT_HALF))
        + hidden * jnp.exp(-0.5 * hidden * hidden) * NORMAL_PEAK
    )
    back_hidden_low = (
        jnp.dot(pulled_low, down_full.T, preferred_element_type=jnp.float32) * slope
    ).astype(jnp.bfloat16)
    grad_up_shift = jnp.sum(back_hidden_low.astype(jnp.float32), axis=0)
    grad_up = jnp.dot(normed_low.T, back_hidden_low, preferred_element_type=jnp.float32)
    back_mixed = jnp.transpose(
        jnp.dot(pulled_low, dense_full.T, preferred_element_type=jnp.float32).reshape(
            local, sequences, HEADS, HEAD_DIM
        ),
        (1, 2, 0, 3),
    )
    scaled_low = (back_mixed / total[..., None]).astype(jnp.bfloat16)
    correction = jnp.sum(back_mixed * mixed, axis=-1) / total
    ready_pairs = lax.all_gather(key_pairs, "ctx", axis=0, tiled=True)

    def slopes_of(piece, start):
        weights, key_part, value_part = exp_weights(piece, start)
        pressure = jnp.einsum(
            "shqd,kshd->shqk", scaled_low, value_part, preferred_element_type=jnp.float32
        )
        slopes_low = (weights * (pressure - correction[..., None])).astype(jnp.bfloat16)
        return (weights, slopes_low, key_part)

    def query_step(carry, piece, start):
        weights, slopes_low, key_part = slopes_of(piece, start)
        return (
            carry
            + jnp.einsum(
                "shqk,kshd->shqd", slopes_low, key_part, preferred_element_type=jnp.float32
            )
            * scale
        )

    back_queries = sweep(
        query_step, jnp.zeros((sequences, HEADS, local, HEAD_DIM), jnp.float32), ready_pairs, 0
    )

    def key_block(start, size):
        piece = lax.dynamic_slice_in_dim(ready_pairs, start, size, 0)
        weights, slopes_low, key_part = slopes_of(piece, start)
        back_keys = (
            jnp.einsum("shqk,qshd->kshd", slopes_low, queries, preferred_element_type=jnp.float32)
            * scale
        )
        back_values = jnp.einsum(
            "shqk,shqd->kshd",
            weights.astype(jnp.bfloat16),
            scaled_low,
            preferred_element_type=jnp.float32,
        )
        return jnp.concatenate(
            [
                back_keys.reshape(size, sequences, width),
                back_values.reshape(size, sequences, width),
            ],
            axis=-1,
        )

    def key_terms(start, count):
        size = math.gcd(count, 512)
        if size == count:
            return key_block(start, count)

        def one_block(turn):
            return key_block(start + turn * size, size)

        blocks = lax.map(one_block, jnp.arange(count // size, dtype=jnp.int32))
        return blocks.reshape(count, sequences, 2 * width)

    pair_grads = lax.psum_scatter(
        key_terms(jnp.int32(0), local * lax.axis_size("ctx")).astype(jnp.bfloat16),
        "ctx",
        scatter_dimension=0,
        tiled=True,
    ).astype(jnp.float32)
    back_key_rows = pair_grads[..., :width].reshape(local, sequences, HEADS, HEAD_DIM)
    back_value_rows = pair_grads[..., width:].reshape(local, sequences, HEADS, HEAD_DIM)
    back_query_rows = jnp.transpose(back_queries, (2, 0, 1, 3))
    back_projected_low = (
        jnp.stack(
            [
                rotary(back_query_rows, cosine, -sine),
                rotary(back_key_rows, cosine, -sine),
                back_value_rows,
            ],
            axis=2,
        )
        .reshape(rows, 3 * width)
        .astype(jnp.bfloat16)
    )
    grad_attend_shift = jnp.sum(back_projected_low.astype(jnp.float32), axis=0)
    grad_attend = jnp.dot(normed_low.T, back_projected_low, preferred_element_type=jnp.float32)
    back_normed = (
        jnp.dot(back_projected_low, attend_full.T, preferred_element_type=jnp.float32)
        + jnp.dot(back_hidden_low, up_full.T, preferred_element_type=jnp.float32)
    ).reshape(local, sequences, width)
    grad_gain = jnp.sum(back_normed * unit, axis=(0, 1))
    grad_shift = jnp.sum(back_normed, axis=(0, 1))
    back_unit = back_normed * gain.astype(jnp.float32)
    back_source = inverse * (
        back_unit
        - jnp.mean(back_unit, axis=-1, keepdims=True)
        - unit * jnp.mean(back_unit * unit, axis=-1, keepdims=True)
    )
    input_grad = (pulled + back_source).astype(jnp.bfloat16)
    terms = (
        grad_gain,
        grad_shift,
        grad_attend,
        grad_attend_shift,
        grad_dense,
        bias_grad,
        grad_up,
        grad_up_shift,
        grad_down,
        bias_grad,
    )
    shards = (
        lax.psum_scatter(
            terms[0].astype(jnp.bfloat16), "dp", scatter_dimension=0, tiled=True
        ).astype(jnp.float32),
        lax.psum_scatter(
            terms[1].astype(jnp.bfloat16), "dp", scatter_dimension=0, tiled=True
        ).astype(jnp.float32),
        lax.psum_scatter(
            terms[2].astype(jnp.bfloat16), "dp", scatter_dimension=0, tiled=True
        ).astype(jnp.float32),
        lax.psum_scatter(
            terms[3].astype(jnp.bfloat16), "dp", scatter_dimension=0, tiled=True
        ).astype(jnp.float32),
        lax.psum_scatter(
            terms[4].astype(jnp.bfloat16), "dp", scatter_dimension=0, tiled=True
        ).astype(jnp.float32),
        lax.psum_scatter(
            terms[5].astype(jnp.bfloat16), "dp", scatter_dimension=0, tiled=True
        ).astype(jnp.float32),
        lax.psum_scatter(
            terms[6].astype(jnp.bfloat16), "dp", scatter_dimension=0, tiled=True
        ).astype(jnp.float32),
        lax.psum_scatter(
            terms[7].astype(jnp.bfloat16), "dp", scatter_dimension=0, tiled=True
        ).astype(jnp.float32),
        lax.psum_scatter(
            terms[8].astype(jnp.bfloat16), "dp", scatter_dimension=0, tiled=True
        ).astype(jnp.float32),
        lax.psum_scatter(
            terms[9].astype(jnp.bfloat16), "dp", scatter_dimension=0, tiled=True
        ).astype(jnp.float32),
    )
    reduced = (
        lax.psum(shards[0].astype(jnp.bfloat16), "ctx").astype(jnp.float32),
        lax.psum(shards[1].astype(jnp.bfloat16), "ctx").astype(jnp.float32),
        lax.psum(shards[2].astype(jnp.bfloat16), "ctx").astype(jnp.float32),
        lax.psum(shards[3].astype(jnp.bfloat16), "ctx").astype(jnp.float32),
        lax.psum(shards[4].astype(jnp.bfloat16), "ctx").astype(jnp.float32),
        lax.psum(shards[5].astype(jnp.bfloat16), "ctx").astype(jnp.float32),
        lax.psum(shards[6].astype(jnp.bfloat16), "ctx").astype(jnp.float32),
        lax.psum(shards[7].astype(jnp.bfloat16), "ctx").astype(jnp.float32),
        lax.psum(shards[8].astype(jnp.bfloat16), "ctx").astype(jnp.float32),
        lax.psum(shards[9].astype(jnp.bfloat16), "ctx").astype(jnp.float32),
    )
    return (
        output,
        input_grad,
        reduced[0],
        reduced[1],
        reduced[2],
        reduced[3],
        reduced[4],
        reduced[5],
        reduced[6],
        reduced[7],
        reduced[8],
        reduced[9],
    )


def solution(mesh):
    return jax.shard_map(
        body,
        mesh=mesh,
        in_specs=(
            P("ctx", "dp", None),
            P("ctx", "dp", None),
            P("dp"),
            P(),
            P("dp"),
            P("dp"),
            P("dp", None),
            P("dp"),
            P("dp", None),
            P("dp"),
            P("dp", None),
            P("dp"),
            P("dp", None),
            P("dp"),
        ),
        out_specs=(
            P("ctx", "dp", None),
            P("ctx", "dp", None),
            P("dp"),
            P("dp"),
            P("dp", None),
            P("dp"),
            P("dp", None),
            P("dp"),
            P("dp", None),
            P("dp"),
            P("dp", None),
            P("dp"),
        ),
        check_vma=False,
    )
```

profile of v0, /device:TPU:0, one launch (start us, length us, event | category | flops | bytes accessed | tf_op | source)
XLA Modules:
  0.0 1102.6 jit_solution(300780800760500734)
XLA Ops:
  8.7 22.8 %all-gather = bf16[8,1,128]{2,1,0:T(2,128)(2,1)S(1)} all-gather(bf16[1,1,128]{2,1,0:T(2,128)(2,1)} %bitcast.110), channel_id=1, replica_groups=mesh['dp'=8,'ctx'=4] {'dp'}, dimensions={0}, use_global_device_ids=true | all-gather | bytes 2304 | tf_op jit(solution)/shard_map/all_gather | solution.py:91
  31.5 17.2 %all-gather.1 = bf16[8,1,128]{2,1,0:T(2,128)(2,1)S(1)} all-gather(bf16[1,1,128]{2,1,0:T(2,128)(2,1)} %bitcast.111), channel_id=1, replica_groups=mesh['dp'=8,'ctx'=4] {'dp'}, dimensions={0}, use_global_device_ids=true | all-gather | bytes 2304 | tf_op jit(solution)/shard_map/all_gather | solution.py:92
  48.7 27.0 %all-gather.2 = bf16[8,1,384]{2,1,0:T(2,128)(2,1)S(1)} all-gather(bf16[1,1,384]{2,1,0:T(2,128)(2,1)S(1)} %reshape.296), channel_id=1, replica_groups=mesh['dp'=8,'ctx'=4] {'dp'}, dimensions={0}, use_global_device_ids=true | all-gather | bytes 6912 | tf_op jit(solution)/shard_map/all_gather | solution.py:94
  82.2 29.6 %all-gather.12.cloned.1.call-done = bf16[1024,3072]{1,0:T(8,128)(2,1)} async-done(((bf16[128,3072]{1,0:T(8,128)(2,1)}), bf16[1024,3072]{1,0:T(8,128)(2,1)}) %all-gather.12.cloned.1.call-update) | async-done | bytes 6291472 | tf_op jit(solution)/shard_map/all_gather | solution.py:93
  111.8 6.3 convolution_add_fusion.1
  118.1 5.7 reshape.283
  123.8 2.8 slice.153
  126.6 4.0 fusion.62
  132.9 3.6 copy.62
  136.5 2.3 copy.63
  146.8 2.3 slice.155
  149.0 27.8 %all-gather.14.cloned.1.call-done = bf16[512,2,2048]{0,2,1:T(8,128)(2,1)} async-done(((bf16[128,2,2048]{0,2,1:T(8,128)(2,1)}), bf16[512,2,2048]{0,2,1:T(8,128)(2,1)}) %all-gather.14.cloned.1.call-update) | async-done | bytes 4194320 | tf_op jit(solution)/shard_map/all_gather | solution.py:160
  176.8 2.5 fusion.63
  182.2 2.7 copy-done.30
  184.9 2.8 fusion.25
  187.7 40.4 %all-gather.16.cloned.1.call-done = bf16[1024,1024]{1,0:T(8,128)(2,1)} async-done(((bf16[128,1024]{1,0:T(8,128)(2,1)}), bf16[1024,1024]{1,0:T(8,128)(2,1)}) %all-gather.16.cloned.1.call-update) | async-done | bytes 2097168 | tf_op jit(solution)/shard_map/all_gather | solution.py:95
  228.1 2.8 multiply_reduce_fusion.3
  231.0 5.1 multiply_convert_fusion
  240.7 6.4 copy.60
  248.7 3.3 copy.52
  252.0 2.6 convert_element_type.188
  254.6 3.1 convolution_convert_fusion.4
  257.8 26.8 %all-gather.4 = bf16[8,1,512]{2,1,0:T(2,128)(2,1)S(1)} all-gather(bf16[1,1,512]{2,1,0:T(2,128)(2,1)S(1)} %reshape.300), channel_id=1, replica_groups=mesh['dp'=8,'ctx'=4] {'dp'}, dimensions={0}, use_global_device_ids=true | all-gather | bytes 9216 | tf_op jit(solution)/shard_map/all_gather | solution.py:98
  284.7 68.7 %all-gather.18.cloned.1.call-done = bf16[1024,4096]{1,0:T(8,128)(2,1)} async-done(((bf16[128,4096]{1,0:T(8,128)(2,1)}), bf16[1024,4096]{1,0:T(8,128)(2,1)}) %all-gather.18.cloned.1.call-update) | async-done | bytes 8388624 | tf_op jit(solution)/shard_map/all_gather | solution.py:97
  353.3 14.5 %fusion.5 = (bf16[256,4096]{1,0:T(8,128)(2,1)S(1)}, f32[256,4096]{1,0:T(8,128)}) fusion(f32[4096]{0:T(1024)S(1)} %bitcast.106, bf16[256,1024]{1,0:T(8,128)(2,1)S(1)} %reshape.282, bf16[1024,4096]{1,0:T(8,128)(2,1)} %all-gather.18.cloned.1.call-done), kind=kOutput, calls=%fused_computation.14 | convolution fusion | flops 2216689664 | bytes 15220736 | tf_op jit(solution)/shard_map/dot_general | solution.py:165
  369.2 5.7 convolution_convert_fusion
  375.3 102.6 %all-gather.20.cloned.1.call-done = bf16[4096,1024]{1,0:T(8,128)(2,1)} async-done(((bf16[512,1024]{1,0:T(8,128)(2,1)}), bf16[4096,1024]{1,0:T(8,128)(2,1)}) %all-gather.20.cloned.1.call-update) | async-done | bytes 8388624 | tf_op jit(solution)/shard_map/all_gather | solution.py:99
  477.9 6.5 fusion.64
  485.8 5.6 convolution_convert_fusion.1
  491.5 3.7 fusion.17
  496.7 26.4 %reduce-scatter.16.cloned.1.call-done = bf16[128,4096]{1,0:T(8,128)(2,1)} async-done(((bf16[512,4096]{1,0:T(8,128)(2,1)}), bf16[128,4096]{1,0:T(8,128)(2,1)}) %reduce-scatter.16.cloned.1.call-update) | async-done | bytes 1048592
  527.5 5.3 copy.54
  532.8 3.2 convert_element_type.200
  536.0 6.0 convolution_convert_fusion.2
  545.1 20.5 %all-gather.3 = bf16[8,1,128]{2,1,0:T(2,128)(2,1)S(1)} all-gather(bf16[1,1,128]{2,1,0:T(2,128)(2,1)S(1)} %bitcast.112), channel_id=1, replica_groups=mesh['dp'=8,'ctx'=4] {'dp'}, dimensions={0}, use_global_device_ids=true | all-gather | bytes 2304 | tf_op jit(solution)/shard_map/all_gather | solution.py:96
  565.6 16.4 %all-gather.5 = bf16[8,1,128]{2,1,0:T(2,128)(2,1)S(1)} all-gather(bf16[1,1,128]{2,1,0:T(2,128)(2,1)S(1)} %bitcast.113), channel_id=1, replica_groups=mesh['dp'=8,'ctx'=4] {'dp'}, dimensions={0}, use_global_device_ids=true | all-gather | bytes 2304 | tf_op jit(solution)/shard_map/all_gather | solution.py:100
  582.1 5.9 fusion.65
  588.0 6.9 fusion.66
  598.5 146.8 %reduce-scatter.14.cloned.1.call-done = bf16[512,1024]{1,0:T(8,128)(2,1)} async-done(((bf16[4096,1024]{1,0:T(8,128)(2,1)}), bf16[512,1024]{1,0:T(8,128)(2,1)}) %reduce-scatter.14.cloned.1.call-update) | async-done | bytes 1048592 | tf_op jit(solution)/shard_map/reduce_scatter | solution.py:329
  745.4 150.3 %reduce-scatter.12.cloned.1.call-done = bf16[128,4096]{1,0:T(8,128)(2,1)} async-done(((bf16[1024,4096]{1,0:T(8,128)(2,1)}), bf16[128,4096]{1,0:T(8,128)(2,1)}) %reduce-scatter.12.cloned.1.call-update) | async-done | bytes 1048592 | tf_op jit(solution)/shard_map/reduce_scatter | solution.py:323
  895.6 120.6 %reduce-scatter.8.cloned.1.call-done = bf16[128,3072]{1,0:T(8,128)(2,1)} async-done(((bf16[1024,3072]{1,0:T(8,128)(2,1)}), bf16[128,3072]{1,0:T(8,128)(2,1)}) %reduce-scatter.8.cloned.1.call-update) | async-done | bytes 786448 | tf_op jit(solution)/shard_map/reduce_scatter | solution.py:311
  1016.2 5.9 fusion.56
  1026.1 35.3 %all-reduce.5 = (bf16[1024]{0:T(1024)(128)(2,1)S(1)}, bf16[1024]{0:T(1024)(128)(2,1)S(1)}, bf16[3072]{0:T(1024)(128)(2,1)S(1)}, bf16[1024]{0:T(1024)(128)(2,1)S(1)}, bf16[4096]{0:T(1024)(128)(2,1)S(1)}) all-reduce(bf16[1024]{0:T(1024)(128)(2,1)S(1)} %get-tuple-element.12, ...), channel_id=3, replica_groups=mesh['dp'=8,'ctx'=4] {'dp'}, use_global_device_ids=true, to_apply=%region_10.11.clone | all-reduce | flops 10240 | bytes 40960
  1061.8 6.5 all-reduce.6
  1070.4 3.3 add_convert_fusion
  1073.7 13.0 %all-reduce.10.cloned.1.call-done = (bf16[128,3072]{1,0:T(8,128)(2,1)}, bf16[128,1024]{1,0:T(8,128)(2,1)}, bf16[128,4096]{1,0:T(8,128)(2,1)}, bf16[512,1024]{1,0:T(8,128)(2,1)}) async-done(((bf16[128,3072]{1,0:T(8,128)(2,1)}, bf16[128,1024]{1,0:T(8,128)(2,1)}, bf16[128,4096]{1,0:T(8,128)(2,1)}, bf16[512,1024]{1,0:T(8,128)(2,1)}), (bf16[128,3072]{1,0:T(8,128)(2,1)}, bf16[128,1024]{1,0:T(8,128)(2,1)}, ...) | async-done | bytes 3145744 | tf_op jit(solution)/shard_map/psum | solution.py:339
  1088.6 2.4 convert_element_type.208
  1091.1 2.8 convert_element_type.214
  (161 shorter events, 51.2 us)
Async XLA Ops:
  7.2 74.2 %copy-start.23 = (s32[8]{0:T(128)S(1)}, s32[8]{0:T(128)}, u32[]{:S(2)}) copy-start(s32[8]{0:T(128)} %param.17) | copy-start | bytes 100
  7.2 104.6 %all-gather.12.cloned.1.call-start = ((), (), s32[]{:S(2)}) async-start(), calls=%async_computation.5 | async-start | bytes 7077888 | tf_op jit(solution)/shard_map/all_gather | solution.py:93
  7.9 168.9 %all-gather.14.cloned.1.call-start = ((), (), s32[]{:S(2)}) async-start(), calls=%async_computation.6 | async-start | bytes 5242880 | tf_op jit(solution)/shard_map/all_gather | solution.py:160
  81.3 403.2 %copy-start.3 = (bf16[256,1024]{1,0:T(8,128)(2,1)}, bf16[256,1024]{1,0:T(8,128)(2,1)S(1)}, u32[]{:S(2)}) copy-start(bf16[256,1024]{1,0:T(8,128)(2,1)S(1)} %reshape.282) | copy-start | bytes 1572868
  141.1 4.5 copy-start.26
  141.2 4.9 copy-start.6
  143.5 84.6 %all-gather.16.cloned.1.call-start = ((), (), s32[]{:S(2)}) async-start(), calls=%async_computation.7 | async-start | bytes 2359296 | tf_op jit(solution)/shard_map/all_gather | solution.py:95
  144.2 209.1 %all-gather.18.cloned.1.call-start = ((), (), s32[]{:S(2)}) async-start(), calls=%async_computation.8 | async-start | bytes 9437184 | tf_op jit(solution)/shard_map/all_gather | solution.py:97
  144.8 333.2 %all-gather.20.cloned.1.call-start = ((), (), s32[]{:S(2)}) async-start(), calls=%async_computation.9 | async-start | bytes 9437184 | tf_op jit(solution)/shard_map/all_gather | solution.py:99
  145.4 377.8 %reduce-scatter.16.cloned.1.call-start = ((), (), s32[]{:S(2)}) async-start(), calls=%async_computation.14 | async-start | bytes 5242880
  146.8 81.3 %copy-start.9 = (bf16[128,2,1024]{2,1,0:T(2,128)(2,1)}, bf16[128,2,1024]{2,1,0:T(2,128)(2,1)S(1)}, u32[]{:S(2)}) copy-start(bf16[128,2,1024]{2,1,0:T(2,128)(2,1)S(1)} %get-tuple-element.31) | copy-start | bytes 1572868
  176.8 2.6 copy-start.15
  179.4 2.3 copy-start.12
  181.6 0.6 copy-start.20
  181.6 3.3 copy-start.30
  228.1 2.8 copy-start.21
  228.1 2.9 copy-start.13
  228.1 8.7 slice-start
  230.9 5.1 copy-start.16
  231.0 5.8 slice-start.1
  236.0 2.4 copy-start
  247.1 351.4 %reduce-scatter.10.cloned.1.call-start = ((), (), s32[]{:S(2)}) async-start(), calls=%async_computation.11 | async-start | bytes 2359296 | tf_op jit(solution)/shard_map/reduce_scatter | solution.py:317
  248.7 9.1 copy-start.22
  257.7 487.6 %reduce-scatter.14.cloned.1.call-start = ((), (), s32[]{:S(2)}) async-start(), calls=%async_computation.13 | async-start | bytes 9437184 | tf_op jit(solution)/shard_map/reduce_scatter | solution.py:329
  367.9 1.3 copy-start.4
  374.9 520.7 %reduce-scatter.12.cloned.1.call-start = ((), (), s32[]{:S(2)}) async-start(), calls=%async_computation.12 | async-start | bytes 9437184 | tf_op jit(solution)/shard_map/reduce_scatter | solution.py:323
  484.5 1.3 copy-start.10
  491.5 524.7 %reduce-scatter.8.cloned.1.call-start = ((), (), s32[]{:S(2)}) async-start(), calls=%async_computation.10 | async-start | bytes 7077888 | tf_op jit(solution)/shard_map/reduce_scatter | solution.py:311
  495.2 29.8 %copy-start.19 = (f32[128,16]{0,1:T(8,128)S(1)}, f32[128,16]{0,1:T(8,128)}, u32[]{:S(2)}) copy-start(f32[128,16]{0,1:T(8,128)} %get-tuple-element.54) | copy-start | bytes 24580
  524.8 0.9 copy-start.18
  524.8 1.1 copy-start.14
  541.9 0.7 copy-start.28
  541.9 3.2 copy-start.24
  541.9 23.7 %copy-start.25 = (bf16[128]{0:T(256)(128)(2,1)S(1)}, bf16[128]{0:T(256)(128)(2,1)}, u32[]{:S(2)}) copy-start(bf16[128]{0:T(256)(128)(2,1)} %param.27) | copy-start | bytes 772
  541.9 40.2 %copy-start.5 = (bf16[256,4096]{1,0:T(8,128)(2,1)S(1)}, bf16[256,4096]{1,0:T(8,128)(2,1)}, u32[]{:S(2)}) copy-start(bf16[256,4096]{1,0:T(8,128)(2,1)} %copy-done.4) | copy-start | bytes 6291460
  542.0 544.8 %all-reduce.10.cloned.1.call-start = ((), (), s32[]{:S(2)}) async-start(), calls=%async_computation.15 | async-start | bytes 6291456 | tf_op jit(solution)/shard_map/psum | solution.py:339
  582.1 5.9 copy-start.11
  588.0 7.0 copy-start.8
  588.0 6.9 copy-start.27
  595.0 421.3 %copy-start.2 = (bf16[256,3072]{1,0:T(8,128)(2,1)S(1)}, bf16[256,3072]{1,0:T(8,128)(2,1)}, u32[]{:S(2)}) copy-start(bf16[256,3072]{1,0:T(8,128)(2,1)} %convert_element_type.200) | copy-start | bytes 4718596
  1016.2 8.2 copy-start.1
  1022.2 48.2 %copy-start.7 = (bf16[128,2,1024]{2,1,0:T(2,128)(2,1)S(1)}, bf16[128,2,1024]{2,1,0:T(2,128)(2,1)}, u32[]{:S(2)}) copy-start(bf16[128,2,1024]{2,1,0:T(2,128)(2,1)} %param.15) | copy-start | bytes 1572868
  1068.7 26.7 %copy-start.29 = (f32[128]{0:T(128)}, f32[128]{0:T(128)S(1)}, u32[]{:S(2)}) copy-start(f32[128]{0:T(128)S(1)} %convert_element_type.212) | copy-start | bytes 1540
  1086.7 7.1 copy-start.17
Sparse Core Ops, SparseCore 0:
  10.2 101.5 all-gather.11
  143.6 33.1 all-gather.13
  179.0 49.0 all-gather.15
  230.0 123.2 all-gather.17
  355.3 122.6 all-gather.19
  480.3 42.7 reduce-scatter.15
  526.7 68.4 reduce-scatter.9
  598.8 146.5 reduce-scatter.13
  749.0 146.5 reduce-scatter.11
  899.1 117.1 reduce-scatter.7
  1018.8 67.8 all-reduce.9
where the time goes:
time: 1110 us; the launch traced here: 1100 us
  waiting for transfers between devices  729 us (66%)
  blocking collectives  173 us (16%)
  matrix products  87.1 us (8%)
  local copies, waits for them, and re-layouts  65.1 us (6%)
  other arithmetic  31.2 us (3%)
  between operations  16.6 us (1%)
    reduce_scatter x1, waiting for transfers between devices, body(): lax.psum_scatter(terms[6].astype(jnp.bfloat16), 'dp', scatter_dimension=0...  150 us
    reduce_scatter x1, waiting for transfers between devices, body(): lax.psum_scatter(terms[8].astype(jnp.bfloat16), 'dp', scatter_dimension=0...  147 us
    reduce_scatter x1, waiting for transfers between devices, body(): lax.psum_scatter(terms[2].astype(jnp.bfloat16), 'dp', scatter_dimension=0...  121 us
    all_gather x1, waiting for transfers between devices, body(): lax.all_gather(down_weight, 'dp', axis=0, tiled=True)  103 us
    all_gather x1, waiting for transfers between devices, body(): lax.all_gather(up_weight, 'dp', axis=0, tiled=True)  68.7 us
    all_gather x1, waiting for transfers between devices, body(): lax.all_gather(dense_weight, 'dp', axis=0, tiled=True)  40.4 us
    unnamed x1, blocking collectives  35.3 us
    all_gather x1, waiting for transfers between devices, body(): lax.all_gather(attend_weight, 'dp', axis=0, tiled=True)  29.6 us
  transfers between devices with their start and end apart: 11, of which 10 were waited for; matrix products, arithmetic and copies ran while one was open for 12% of the time, Pallas kernels for 0%

commit v1 on v0

--- a/solution.py
+++ b/solution.py
@@ -11,6 +11,22 @@
 EPSILON = 1e-05
 ROOT_HALF = 0.7071067811865476
 NORMAL_PEAK = 0.3989422804014327
+
+
+def ring_gather(x, axis, dim):
+    ways, here, lap = (lax.axis_size(axis), lax.axis_index(axis), x.shape[dim])
+    shape = [n * ways if d == dim else n for d, n in enumerate(x.shape)]
+    full = lax.dynamic_update_slice_in_dim(jnp.zeros(shape, x.dtype), x, here * lap, axis=dim)
+    going_up = going_down = x
+    for far in range(1, ways // 2 + 1):
+        going_up = lax.ppermute(going_up, axis, [(d, (d + 1) % ways) for d in range(ways)])
+        full = lax.dynamic_update_slice_in_dim(full, going_up, (here - far) % ways * lap, axis=dim)
+        if 2 * far < ways:
+            going_down = lax.ppermute(going_down, axis, [(d, (d - 1) % ways) for d in range(ways)])
+            full = lax.dynamic_update_slice_in_dim(
+                full, going_down, (here + far) % ways * lap, axis=dim
+            )
+    return full
 
 
 def place_of(block_order, first_slot, count):
@@ -90,7 +106,7 @@
     ) = (
         lax.all_gather(norm_gain, "dp", axis=0, tiled=True),
         lax.all_gather(norm_bias, "dp", axis=0, tiled=True),
-        lax.all_gather(attend_weight, "dp", axis=0, tiled=True),
+        ring_gather(attend_weight, "dp", 0),
         lax.all_gather(attend_bias, "dp", axis=0, tiled=True),
         lax.all_gather(dense_weight, "dp", axis=0, tiled=True),
         lax.all_gather(dense_bias, "dp", axis=0, tiled=True),

time: 1110 us -> 1200 us (1.081)
  waiting for transfers between devices: 729 us -> 787 us
  blocking collectives: 173 us -> 191 us
  starting transfers between devices: 1.23 us -> 18.2 us
    ppermute x0 -> x7, waiting for transfers between devices: none -> 64.2 us  [the longest x4 62.7 us: ring_gather(): lax.ppermute(going_up, axis, [(d, (d + 1) % ways) for d in range(ways)])]
    all_gather x1 -> x0, waiting for transfers between devices: 29.6 us -> none  [body(): lax.all_gather(attend_weight, 'dp', axis=0, tiled=True)]
    all_gather x1, blocking collectives: 22.8 us -> 41.9 us  [body(): lax.all_gather(norm_gain, 'dp', axis=0, tiled=True)]
    ppermute x0 -> x7, starting transfers between devices: none -> 17.4 us  [the longest x3 10.2 us: ring_gather(): lax.ppermute(going_down, axis, [(d, (d - 1) % ways) for d in range(ways)])]
    unnamed x12 -> x11, waiting for transfers between devices: 28.9 us -> 30.5 us
  transfers between devices with their start and end apart: 11 -> 17, of which waited for: 10 -> 15; matrix products, arithmetic and copies ran while one was open for 12% -> 10% of each run, Pallas kernels for 0% -> 0%
where the time goes in v1:
time: 1200 us; the launch traced here: 1190 us
  waiting for transfers between devices  787 us (66%)
  blocking collectives  191 us (16%)
  matrix products  80.7 us (7%)
  local copies, waits for them, and re-layouts  64.7 us (5%)
  other arithmetic  32.7 us (3%)
  starting transfers between devices  18.2 us (2%)
  between operations  17.1 us (1%)
    reduce_scatter x1, waiting for transfers between devices, body(): lax.psum_scatter(terms[8].astype(jnp.bfloat16), 'dp', scatter_dimension=0...  150 us
    reduce_scatter x1, waiting for transfers between devices, body(): lax.psum_scatter(terms[6].astype(jnp.bfloat16), 'dp', scatter_dimension=0...  150 us
    reduce_scatter x1, waiting for transfers between devices, body(): lax.psum_scatter(terms[2].astype(jnp.bfloat16), 'dp', scatter_dimension=0...  121 us
    all_gather x1, waiting for transfers between devices, body(): lax.all_gather(down_weight, 'dp', axis=0, tiled=True)  104 us
    all_gather x1, waiting for transfers between devices, body(): lax.all_gather(up_weight, 'dp', axis=0, tiled=True)  79.1 us
    ppermute x4, waiting for transfers between devices, ring_gather(): lax.ppermute(going_up, axis, [(d, (d + 1) % ways) for d in range(ways)])  62.7 us
    all_gather x1, blocking collectives, body(): lax.all_gather(norm_gain, 'dp', axis=0, tiled=True)  41.9 us
    all_gather x1, waiting for transfers between devices, body(): lax.all_gather(dense_weight, 'dp', axis=0, tiled=True)  40.4 us
  transfers between devices with their start and end apart: 17, of which 15 were waited for; matrix products, arithmetic and copies ran while one was open for 10% of the time, Pallas kernels for 0%

profile of v1, /device:TPU:0, one launch (start us, length us, event | category | flops | bytes accessed | tf_op | source)
XLA Modules:
  0.0 1192.1 jit_solution(2513914126929263583)
XLA Ops:
  7.2 6.1 collective-permute-start.1
  17.5 41.9 %all-gather = bf16[8,1,128]{2,1,0:T(2,128)(2,1)S(1)} all-gather(bf16[1,1,128]{2,1,0:T(2,128)(2,1)} %bitcast.110), channel_id=1, replica_groups=mesh['dp'=8,'ctx'=4] {'dp'}, dimensions={0}, use_global_device_ids=true | all-gather | bytes 2304 | tf_op jit(solution)/shard_map/all_gather | solution.py:107
  59.4 16.5 %all-gather.1 = bf16[8,1,128]{2,1,0:T(2,128)(2,1)S(1)} all-gather(bf16[1,1,128]{2,1,0:T(2,128)(2,1)} %bitcast.111), channel_id=1, replica_groups=mesh['dp'=8,'ctx'=4] {'dp'}, dimensions={0}, use_global_device_ids=true | all-gather | bytes 2304 | tf_op jit(solution)/shard_map/all_gather | solution.py:108
  78.7 28.6 %all-gather.2 = bf16[8,1,384]{2,1,0:T(2,128)(2,1)S(1)} all-gather(bf16[1,1,384]{2,1,0:T(2,128)(2,1)S(1)} %reshape.296), channel_id=1, replica_groups=mesh['dp'=8,'ctx'=4] {'dp'}, dimensions={0}, use_global_device_ids=true | all-gather | bytes 6912 | tf_op jit(solution)/shard_map/all_gather | solution.py:110
  114.1 29.3 %collective-permute-done.2 = bf16[128,3072]{1,0:T(8,128)(2,1)S(1)} collective-permute-done((bf16[128,3072]{1,0:T(8,128)(2,1)}, bf16[128,3072]{1,0:T(8,128)(2,1)S(1)}, u32[]{:S(2)}, u32[]{:S(2)}) %collective-permute-start.2) | collective-permute-done | bytes 786464 | tf_op jit(solution)/shard_map/ppermute | solution.py:22
  149.5 22.0 %collective-permute-done.4 = bf16[128,3072]{1,0:T(8,128)(2,1)S(1)} collective-permute-done((bf16[128,3072]{1,0:T(8,128)(2,1)S(1)}, bf16[128,3072]{1,0:T(8,128)(2,1)S(1)}, u32[]{:S(2)}, u32[]{:S(2)}) %collective-permute-start.4) | collective-permute-done | bytes 786464 | tf_op jit(solution)/shard_map/ppermute | solution.py:22
  175.0 11.4 collective-permute-done.6
  186.5 2.6 copy-done.2
  189.0 3.6 convolution_add_fusion.1
  192.6 5.7 reshape.283
  200.1 4.0 fusion.62
  206.1 2.7 copy.62
  219.2 30.2 %all-gather.11.cloned.1.call-done = bf16[512,2,2048]{0,2,1:T(8,128)(2,1)} async-done(((bf16[128,2,2048]{0,2,1:T(8,128)(2,1)}), bf16[512,2,2048]{0,2,1:T(8,128)(2,1)}) %all-gather.11.cloned.1.call-update) | async-done | bytes 4194320 | tf_op jit(solution)/shard_map/all_gather | solution.py:176
  249.4 2.5 fusion.63
  254.1 3.3 copy-done.31
  257.4 2.8 fusion.25
  260.2 40.4 %all-gather.13.cloned.1.call-done = bf16[1024,1024]{1,0:T(8,128)(2,1)} async-done(((bf16[128,1024]{1,0:T(8,128)(2,1)}), bf16[1024,1024]{1,0:T(8,128)(2,1)}) %all-gather.13.cloned.1.call-update) | async-done | bytes 2097168 | tf_op jit(solution)/shard_map/all_gather | solution.py:111
  300.6 2.8 multiply_reduce_fusion.3
  306.6 2.7 multiply_convert_fusion
  310.1 2.5 pad_maximum_fusion
  312.6 6.4 copy.60
  320.7 3.5 copy.52
  328.3 3.8 fusion.17
  333.7 28.7 %reduce-scatter.16.cloned.1.call-done = bf16[128,4096]{1,0:T(8,128)(2,1)} async-done(((bf16[512,4096]{1,0:T(8,128)(2,1)}), bf16[128,4096]{1,0:T(8,128)(2,1)}) %reduce-scatter.16.cloned.1.call-update) | async-done | bytes 1048592
  366.7 5.3 copy.54
  372.0 3.2 convert_element_type.200
  375.1 6.0 convolution_convert_fusion.2
  381.8 28.1 %all-gather.4 = bf16[8,1,512]{2,1,0:T(2,128)(2,1)S(1)} all-gather(bf16[1,1,512]{2,1,0:T(2,128)(2,1)S(1)} %reshape.300), channel_id=1, replica_groups=mesh['dp'=8,'ctx'=4] {'dp'}, dimensions={0}, use_global_device_ids=true | all-gather | bytes 9216 | tf_op jit(solution)/shard_map/all_gather | solution.py:114
  410.0 79.1 %all-gather.15.cloned.1.call-done = bf16[1024,4096]{1,0:T(8,128)(2,1)} async-done(((bf16[128,4096]{1,0:T(8,128)(2,1)}), bf16[1024,4096]{1,0:T(8,128)(2,1)}) %all-gather.15.cloned.1.call-update) | async-done | bytes 8388624 | tf_op jit(solution)/shard_map/all_gather | solution.py:113
  489.1 14.5 %fusion.5 = (bf16[256,4096]{1,0:T(8,128)(2,1)S(1)}, f32[256,4096]{1,0:T(8,128)}) fusion(f32[4096]{0:T(1024)S(1)} %bitcast.106, bf16[256,1024]{1,0:T(8,128)(2,1)S(1)} %copy-done.5, bf16[1024,4096]{1,0:T(8,128)(2,1)} %all-gather.15.cloned.1.call-done), kind=kOutput, calls=%fused_computation.14 | convolution fusion | flops 2216689664 | bytes 15220736 | tf_op jit(solution)/shard_map/dot_general | solution.py:181
  503.7 5.7 convolution_convert_fusion
  509.4 104.4 %all-gather.17.cloned.1.call-done = bf16[4096,1024]{1,0:T(8,128)(2,1)} async-done(((bf16[512,1024]{1,0:T(8,128)(2,1)}), bf16[4096,1024]{1,0:T(8,128)(2,1)}) %all-gather.17.cloned.1.call-update) | async-done | bytes 8388624 | tf_op jit(solution)/shard_map/all_gather | solution.py:115
  613.8 6.6 fusion.64
  621.7 5.6 convolution_convert_fusion.1
  630.5 17.7 %all-gather.3 = bf16[8,1,128]{2,1,0:T(2,128)(2,1)S(1)} all-gather(bf16[1,1,128]{2,1,0:T(2,128)(2,1)S(1)} %bitcast.112), channel_id=1, replica_groups=mesh['dp'=8,'ctx'=4] {'dp'}, dimensions={0}, use_global_device_ids=true | all-gather | bytes 2304 | tf_op jit(solution)/shard_map/all_gather | solution.py:112
  648.2 17.1 %all-gather.5 = bf16[8,1,128]{2,1,0:T(2,128)(2,1)S(1)} all-gather(bf16[1,1,128]{2,1,0:T(2,128)(2,1)S(1)} %bitcast.113), channel_id=1, replica_groups=mesh['dp'=8,'ctx'=4] {'dp'}, dimensions={0}, use_global_device_ids=true | all-gather | bytes 2304 | tf_op jit(solution)/shard_map/all_gather | solution.py:116
  665.3 5.9 fusion.65
  672.5 7.5 fusion.66
  680.1 4.3 reduce-scatter.10.cloned.1.call-done
  684.4 120.6 %reduce-scatter.8.cloned.1.call-done = bf16[128,3072]{1,0:T(8,128)(2,1)} async-done(((bf16[1024,3072]{1,0:T(8,128)(2,1)}), bf16[128,3072]{1,0:T(8,128)(2,1)}) %reduce-scatter.8.cloned.1.call-update) | async-done | bytes 786448 | tf_op jit(solution)/shard_map/reduce_scatter | solution.py:327
  805.0 150.4 %reduce-scatter.14.cloned.1.call-done = bf16[512,1024]{1,0:T(8,128)(2,1)} async-done(((bf16[4096,1024]{1,0:T(8,128)(2,1)}), bf16[512,1024]{1,0:T(8,128)(2,1)}) %reduce-scatter.14.cloned.1.call-update) | async-done | bytes 1048592 | tf_op jit(solution)/shard_map/reduce_scatter | solution.py:345
  955.5 150.3 %reduce-scatter.12.cloned.1.call-done = bf16[128,4096]{1,0:T(8,128)(2,1)} async-done(((bf16[1024,4096]{1,0:T(8,128)(2,1)}), bf16[128,4096]{1,0:T(8,128)(2,1)}) %reduce-scatter.12.cloned.1.call-update) | async-done | bytes 1048592 | tf_op jit(solution)/shard_map/reduce_scatter | solution.py:339
  1105.8 5.9 fusion.56
  1115.8 34.9 %all-reduce.5 = (bf16[1024]{0:T(1024)(128)(2,1)S(1)}, bf16[1024]{0:T(1024)(128)(2,1)S(1)}, bf16[3072]{0:T(1024)(128)(2,1)S(1)}, bf16[1024]{0:T(1024)(128)(2,1)S(1)}, bf16[4096]{0:T(1024)(128)(2,1)S(1)}) all-reduce(bf16[1024]{0:T(1024)(128)(2,1)S(1)} %get-tuple-element.12, ...), channel_id=3, replica_groups=mesh['dp'=8,'ctx'=4] {'dp'}, use_global_device_ids=true, to_apply=%region_10.11.clone | all-reduce | flops 10240 | bytes 40960
  1151.1 6.5 all-reduce.6
  1159.7 3.3 add_convert_fusion
  1163.0 12.9 %all-reduce.10.cloned.1.call-done = (bf16[128,3072]{1,0:T(8,128)(2,1)}, bf16[128,1024]{1,0:T(8,128)(2,1)}, bf16[128,4096]{1,0:T(8,128)(2,1)}, bf16[512,1024]{1,0:T(8,128)(2,1)}) async-done(((bf16[128,3072]{1,0:T(8,128)(2,1)}, bf16[128,1024]{1,0:T(8,128)(2,1)}, bf16[128,4096]{1,0:T(8,128)(2,1)}, bf16[512,1024]{1,0:T(8,128)(2,1)}), (bf16[128,3072]{1,0:T(8,128)(2,1)}, bf16[128,1024]{1,0:T(8,128)(2,1)}, ...) | async-done | bytes 3145744 | tf_op jit(solution)/shard_map/psum | solution.py:355
  1180.2 2.8 convert_element_type.214
  (180 shorter events, 72.7 us)
Async XLA Ops:
  7.2 242.2 %all-gather.11.cloned.1.call-start = ((), (), s32[]{:S(2)}) async-start(), calls=%async_computation.5 | async-start | bytes 5242880 | tf_op jit(solution)/shard_map/all_gather | solution.py:176
  7.2 103.7 %collective-permute-start.1 = (bf16[128,3072]{1,0:T(8,128)(2,1)}, bf16[128,3072]{1,0:T(8,128)(2,1)S(1)}, u32[]{:S(2)}, u32[]{:S(2)}) collective-permute-start(bf16[128,3072]{1,0:T(8,128)(2,1)} %param.20), channel_id=1, source_target_pairs={{0,28},{4,0},{8,4},{12,8},{16,12},{20,16},{24,20},{28,24},{1,29},{... | collective-permute-start | bytes 2359304 | tf_op jit(solution)/shard_map/ppermute | solution.py:25
  13.3 94.3 %collective-permute-start = (bf16[128,3072]{1,0:T(8,128)(2,1)}, bf16[128,3072]{1,0:T(8,128)(2,1)}, u32[]{:S(2)}, u32[]{:S(2)}) collective-permute-start(bf16[128,3072]{1,0:T(8,128)(2,1)} %param.20), channel_id=1, source_target_pairs={{0,4},{4,8},{8,12},{12,16},{16,20},{20,24},{24,28},{28,0},{1,5},{5... | collective-permute-start | bytes 2359304 | tf_op jit(solution)/shard_map/ppermute | solution.py:22
  75.9 35.0 %copy-start.20 = (bf16[128,3072]{1,0:T(8,128)(2,1)S(1)}, bf16[128,3072]{1,0:T(8,128)(2,1)}, u32[]{:S(2)}) copy-start(bf16[128,3072]{1,0:T(8,128)(2,1)} %param.20) | copy-start | bytes 2359300
  107.6 78.9 %copy-start.4 = (bf16[256,1024]{1,0:T(8,128)(2,1)}, bf16[256,1024]{1,0:T(8,128)(2,1)S(1)}, u32[]{:S(2)}) copy-start(bf16[256,1024]{1,0:T(8,128)(2,1)S(1)} %reshape.282) | copy-start | bytes 1572868
  107.6 35.7 %collective-permute-start.2 = (bf16[128,3072]{1,0:T(8,128)(2,1)}, bf16[128,3072]{1,0:T(8,128)(2,1)S(1)}, u32[]{:S(2)}, u32[]{:S(2)}) collective-permute-start(bf16[128,3072]{1,0:T(8,128)(2,1)} %collective-permute-done), channel_id=1, source_target_pairs={{0,4},{4,8},{8,12},{12,16},{16,20},{20,24},{24,28},{28,0},{1,5},{5... | collective-permute-start | bytes 2359304 | tf_op jit(solution)/shard_map/ppermute | solution.py:22
  111.0 36.8 %collective-permute-start.3 = (bf16[128,3072]{1,0:T(8,128)(2,1)S(1)}, bf16[128,3072]{1,0:T(8,128)(2,1)S(1)}, u32[]{:S(2)}, u32[]{:S(2)}) collective-permute-start(bf16[128,3072]{1,0:T(8,128)(2,1)S(1)} %collective-permute-done.1), channel_id=1, source_target_pairs={{0,28},{4,0},{8,4},{12,8},{16,12},{20,16},{24,20},{28,24},{1,29},{... | collective-permute-start | bytes 2359304 | tf_op jit(solution)/shard_map/ppermute | solution.py:25
  143.3 28.1 %collective-permute-start.4 = (bf16[128,3072]{1,0:T(8,128)(2,1)S(1)}, bf16[128,3072]{1,0:T(8,128)(2,1)S(1)}, u32[]{:S(2)}, u32[]{:S(2)}) collective-permute-start(bf16[128,3072]{1,0:T(8,128)(2,1)S(1)} %collective-permute-done.2), channel_id=1, source_target_pairs={{0,4},{4,8},{8,12},{12,16},{16,20},{20,24},{24,28},{28,0},{1,5},{5... | collective-permute-start | bytes 2359304 | tf_op jit(solution)/shard_map/ppermute | solution.py:22
  147.7 27.1 %collective-permute-start.5 = (bf16[128,3072]{1,0:T(8,128)(2,1)S(1)}, bf16[128,3072]{1,0:T(8,128)(2,1)S(1)}, u32[]{:S(2)}, u32[]{:S(2)}) collective-permute-start(bf16[128,3072]{1,0:T(8,128)(2,1)S(1)} %collective-permute-done.3), channel_id=1, source_target_pairs={{0,28},{4,0},{8,4},{12,8},{16,12},{20,16},{24,20},{28,24},{1,29},{... | collective-permute-start | bytes 2359304 | tf_op jit(solution)/shard_map/ppermute | solution.py:25
  171.5 14.9 %collective-permute-start.6 = (bf16[128,3072]{1,0:T(8,128)(2,1)S(1)}, bf16[128,3072]{1,0:T(8,128)(2,1)S(1)}, u32[]{:S(2)}, u32[]{:S(2)}) collective-permute-start(bf16[128,3072]{1,0:T(8,128)(2,1)S(1)} %collective-permute-done.4), channel_id=1, source_target_pairs={{0,4},{4,8},{8,12},{12,16},{16,20},{20,24},{24,28},{28,0},{1,5},{5... | collective-permute-start | bytes 2359304 | tf_op jit(solution)/shard_map/ppermute | solution.py:22
  186.4 2.6 copy-start.2
  211.0 3.4 copy-start.13
  211.0 5.5 copy-start.27
  211.0 5.7 copy-start.24
  211.0 5.9 copy-start.8
  215.5 85.1 %all-gather.13.cloned.1.call-start = ((), (), s32[]{:S(2)}) async-start(), calls=%async_computation.6 | async-start | bytes 2359296 | tf_op jit(solution)/shard_map/all_gather | solution.py:111
  216.2 146.1 %reduce-scatter.16.cloned.1.call-start = ((), (), s32[]{:S(2)}) async-start(), calls=%async_computation.13 | async-start | bytes 5242880
  219.2 32.7 %copy-start.18 = (bf16[128,2,16,48]{0,3,2,1:T(8,128)(2,1)S(1)}, bf16[128,2,16,48]{0,3,2,1:T(8,128)(2,1)}, u32[]{:S(2)}) copy-start(bf16[128,2,16,48]{0,3,2,1:T(8,128)(2,1)} %slice.155) | copy-start | bytes 1179652
  251.9 2.3 copy-start.15
  254.1 3.3 copy-start.31
  257.4 43.2 %copy-start.12 = (bf16[128,2,1024]{2,1,0:T(2,128)(2,1)S(1)}, bf16[128,2,1024]{2,1,0:T(2,128)(2,1)}, u32[]{:S(2)}) copy-start(bf16[128,2,1024]{2,1,0:T(2,128)(2,1)} %get-tuple-element.31) | copy-start | bytes 1572868
  300.6 4.3 copy-start.32
  304.9 1.7 copy-start.16
  309.3 3.3 copy-start
  319.1 170.1 %all-gather.15.cloned.1.call-start = ((), (), s32[]{:S(2)}) async-start(), calls=%async_computation.7 | async-start | bytes 9437184 | tf_op jit(solution)/shard_map/all_gather | solution.py:113
  319.6 294.1 %all-gather.17.cloned.1.call-start = ((), (), s32[]{:S(2)}) async-start(), calls=%async_computation.8 | async-start | bytes 9437184 | tf_op jit(solution)/shard_map/all_gather | solution.py:115
  320.2 364.2 %reduce-scatter.10.cloned.1.call-start = ((), (), s32[]{:S(2)}) async-start(), calls=%async_computation.10 | async-start | bytes 2359296 | tf_op jit(solution)/shard_map/reduce_scatter | solution.py:333
  320.7 7.6 copy-start.6
  326.2 2.1 copy-start.10
  328.3 476.8 %reduce-scatter.8.cloned.1.call-start = ((), (), s32[]{:S(2)}) async-start(), calls=%async_computation.9 | async-start | bytes 7077888 | tf_op jit(solution)/shard_map/reduce_scatter | solution.py:327
  332.2 32.0 %copy-start.22 = (f32[128,16]{0,1:T(8,128)S(1)}, f32[128,16]{0,1:T(8,128)}, u32[]{:S(2)}) copy-start(f32[128,16]{0,1:T(8,128)} %get-tuple-element.54) | copy-start | bytes 24580
  363.9 0.9 copy-start.21
  364.0 1.1 copy-start.17
  381.1 108.0 %copy-start.5 = (bf16[256,1024]{1,0:T(8,128)(2,1)S(1)}, bf16[256,1024]{1,0:T(8,128)(2,1)}, u32[]{:S(2)}) copy-start(bf16[256,1024]{1,0:T(8,128)(2,1)} %copy-done.4) | copy-start | bytes 1572868
  381.2 574.3 %reduce-scatter.14.cloned.1.call-start = ((), (), s32[]{:S(2)}) async-start(), calls=%async_computation.12 | async-start | bytes 9437184 | tf_op jit(solution)/shard_map/reduce_scatter | solution.py:345
  489.1 14.5 %copy-start.7 = (bf16[256,1024]{1,0:T(8,128)(2,1)S(1)}, bf16[256,1024]{1,0:T(8,128)(2,1)}, u32[]{:S(2)}) copy-start(bf16[256,1024]{1,0:T(8,128)(2,1)} %copy-done.6) | copy-start | bytes 1572868
  509.4 596.4 %reduce-scatter.12.cloned.1.call-start = ((), (), s32[]{:S(2)}) async-start(), calls=%async_computation.11 | async-start | bytes 9437184 | tf_op jit(solution)/shard_map/reduce_scatter | solution.py:339
  620.4 1.3 copy-start.14
  627.3 3.2 copy-start.25
  627.3 20.9 %copy-start.26 = (bf16[128]{0:T(256)(128)(2,1)S(1)}, bf16[128]{0:T(256)(128)(2,1)}, u32[]{:S(2)}) copy-start(bf16[128]{0:T(256)(128)(2,1)} %param.27) | copy-start | bytes 772
  627.3 548.6 %all-reduce.10.cloned.1.call-start = ((), (), s32[]{:S(2)}) async-start(), calls=%async_computation.14 | async-start | bytes 6291456 | tf_op jit(solution)/shard_map/psum | solution.py:355
  665.3 5.9 copy-start.11
  665.3 5.9 copy-start.28
  672.5 433.2 %copy-start.3 = (bf16[256,3072]{1,0:T(8,128)(2,1)S(1)}, bf16[256,3072]{1,0:T(8,128)(2,1)}, u32[]{:S(2)}) copy-start(bf16[256,3072]{1,0:T(8,128)(2,1)} %convert_element_type.200) | copy-start | bytes 4718596
  1105.8 8.3 copy-start.1
  1111.7 48.0 %copy-start.9 = (bf16[128,2,1024]{2,1,0:T(2,128)(2,1)S(1)}, bf16[128,2,1024]{2,1,0:T(2,128)(2,1)}, u32[]{:S(2)}) copy-start(bf16[128,2,1024]{2,1,0:T(2,128)(2,1)} %param.15) | copy-start | bytes 1572868
  1158.0 26.5 %copy-start.30 = (f32[128]{0:T(128)}, f32[128]{0:T(128)S(1)}, u32[]{:S(2)}) copy-start(f32[128]{0:T(128)S(1)} %convert_element_type.212) | copy-start | bytes 1540
  1175.9 7.1 copy-start.19
  (2 other events, 1.3 us)
Sparse Core Ops, SparseCore 0:
  215.6 33.7 all-gather.10
  251.5 49.0 all-gather.12
  319.2 43.1 reduce-scatter.15
  364.3 124.7 all-gather.14
  491.1 122.6 all-gather.16
  617.7 66.6 reduce-scatter.9
  688.0 117.0 reduce-scatter.7
  808.7 146.7 reduce-scatter.13
  959.1 146.5 reduce-scatter.11
  1108.2 67.7 all-reduce.9
